TPU v7x, 32 devices: a whole 2x2x4 slice. The times are simulated.
32 devices in a mesh: node: 16 (over z, y, x), rep: 2 (over core).
Axes of the slice: x: 2, y: 2, z: 4, core: 2. Of those that a mesh axis runs over, the one named last changes fastest.
Arguments:
- features: bfloat16 [4096, 512], P(('rep', 'node')), parts along dimension 0, may hold values from -24 to 24
- upstream: bfloat16 [4096, 512], P(('rep', 'node')), parts along dimension 0, may hold values from -36 to 36
- weight_one: bfloat16 [512, 512], replicated, may hold values from -0.25 to 0.25
- weight_two: bfloat16 [512, 512], replicated, may hold values from -0.25 to 0.25
- neighbours: int32 [4096, 32], P(('rep', 'node')), parts along dimension 0, may hold values from 0 to 2047, as said below
- edge_weight: int32 [4096, 32], P(('rep', 'node')), parts along dimension 0, may hold values from 1 to 8
- fetch_block: int32 [512, 2], P('rep'), parts along dimension 0, may hold values from 0 to 15, as said below
- fetch_count: int32 [512], P('rep'), parts along dimension 0, may hold values from 0 to 2, as said below
Outputs:
- d_features: bfloat16 [4096, 512], P(('rep', 'node')), parts along dimension 0
- grad_one: bfloat16 [1024, 512], P('rep'), parts along dimension 0
- grad_two: bfloat16 [1024, 512], P('rep'), parts along dimension 0
There are 2 independent parts, one for each index of `rep`. A program takes and returns all parts, laid end to end along the dimension named above; an argument that names none is the same for every part. Nothing has to cross between parts.
Inputs may be any that keep to these rules, and one draw needn't show every extreme that they name: `neighbours`: no node names itself. `fetch_block`: the 2 blocks listed for one pair of devices are distinct. `fetch_count`: zero where p = d; every device has 2 live blocks from some other device.
All inputs are finite; a program needn't handle non-finite values.
Results may differ from a plain program's by a relative error of at most 0.013.
Values may be sent and summed in bfloat16 or wider, within the bound.
No kernel may reach another device: no remote copies, remote signals or barrier semaphores. Data moves between devices by JAX's collectives and lax.ppermute only.
A program may use at most 64 MiB of HBM per device.

v0:
```python
import math
import jax
import jax.numpy as jnp
from jax import lax
from jax.sharding import PartitionSpec as P

D = 512
ROWS = 128
HALO = 32
BLK = 8
CAP = 2
SELF_WEIGHT = 8.0


def with_halo(block, sides, width):
    for axis, dim in sides:
        count = lax.axis_size(axis)
        forward = [(i, i + 1) for i in range(count - 1)]
        backward = [(target, source) for source, target in forward]
        low = lax.ppermute(
            lax.slice_in_dim(block, block.shape[dim] - width, None, axis=dim), axis, forward
        )
        high = lax.ppermute(lax.slice_in_dim(block, 0, width, axis=dim), axis, backward)
        block = jnp.concatenate([low, block, high], axis=dim)
    return block


def gelu_tanh(values):
    return jax.nn.gelu(values, approximate=True)


def edge_tables(neighbours, edge_weight, fetch_block, fetch_count, peer_count, device):
    first_row = device * ROWS
    local_rows = jnp.arange(ROWS, dtype=jnp.int32)
    owner_dev = neighbours // ROWS
    in_band = (neighbours >= first_row - HALO) & (neighbours < first_row + ROWS + HALO)
    my_table = lax.dynamic_slice_in_dim(fetch_block, device * peer_count, peer_count, 0)
    my_counts = lax.dynamic_slice_in_dim(fetch_count, device * peer_count, peer_count, 0)
    target = neighbours % ROWS // BLK
    listed = jnp.take(my_table, owner_dev, axis=0)
    live_slot = (
        jnp.arange(CAP, dtype=jnp.int32)[None, None, :] < jnp.take(my_counts, owner_dev)[..., None]
    )
    matched = (listed == target[..., None]) & live_slot
    found_slot = jnp.any(matched, axis=-1)
    slot_index = jnp.argmax(matched, axis=-1)
    weight = edge_weight.astype(jnp.float32)
    band_weight = jnp.where(in_band, weight, 0.0)
    far_use = jnp.logical_not(in_band) & found_slot
    far_weight = jnp.where(far_use, weight, 0.0)
    band_col = jnp.where(in_band, neighbours - first_row + HALO, 0)
    far_col = jnp.where(far_use, (owner_dev * CAP + slot_index) * BLK + neighbours % BLK, 0)
    row_index = jnp.broadcast_to(local_rows[:, None], neighbours.shape)
    band_matrix = (
        jnp.zeros((ROWS, ROWS + 2 * HALO), jnp.float32).at[row_index, band_col].add(band_weight)
    )
    band_matrix = band_matrix.at[local_rows, local_rows + HALO].add(SELF_WEIGHT)
    far_matrix = (
        jnp.zeros((ROWS, peer_count * CAP * BLK), jnp.float32)
        .at[row_index, far_col]
        .add(far_weight)
    )
    row_total = SELF_WEIGHT + jnp.sum(band_weight + far_weight, axis=1)
    asked_blocks = jnp.take(
        fetch_block, jnp.arange(peer_count, dtype=jnp.int32) * peer_count + device, axis=0
    )
    return (
        band_matrix.astype(jnp.bfloat16),
        far_matrix.astype(jnp.bfloat16),
        row_total,
        asked_blocks,
    )


def aggregate(values, band_matrix, far_matrix, row_total, asked_blocks):
    extended = with_halo(values, (("node", 0),), HALO)
    outgoing = values.reshape(ROWS // BLK, BLK, D)[asked_blocks]
    incoming = lax.all_to_all(outgoing, "node", split_axis=0, concat_axis=0, tiled=True)
    sums = jnp.dot(band_matrix, extended, preferred_element_type=jnp.float32)
    sums = sums + jnp.dot(far_matrix, incoming.reshape(-1, D), preferred_element_type=jnp.float32)
    return (sums / row_total[:, None]).astype(jnp.bfloat16)


def adjoint(cotangent, band_matrix, far_matrix, asked_blocks, peer_count):
    back_band = lax.dot_general(
        band_matrix, cotangent, (((0,), (0,)), ((), ())), preferred_element_type=jnp.float32
    )
    own_rows = back_band[HALO : HALO + ROWS]
    rim_terms = jnp.concatenate([back_band[:HALO], back_band[HALO + ROWS :]], axis=0)
    rim_back = with_halo(rim_terms.astype(jnp.bfloat16), (("node", 0),), HALO).astype(
        rim_terms.dtype
    )
    own_rows = own_rows.at[:HALO].add(rim_back[:HALO])
    own_rows = own_rows.at[ROWS - HALO :].add(rim_back[3 * HALO :])
    back_far = lax.dot_general(
        far_matrix, cotangent, (((0,), (0,)), ((), ())), preferred_element_type=jnp.float32
    )
    back_far = back_far.reshape(peer_count, CAP, BLK, D)
    returned = lax.all_to_all(
        back_far.astype(jnp.bfloat16), "node", split_axis=0, concat_axis=0, tiled=True
    ).astype(back_far.dtype)
    own_rows = own_rows.reshape(ROWS // BLK, BLK, D).at[asked_blocks].add(returned)
    return own_rows.reshape(ROWS, D)


def contract_rows(left, right):
    return lax.dot_general(
        left, right, (((0,), (0,)), ((), ())), preferred_element_type=jnp.float32
    )


def sum_weight_grad(partial_grad):
    return lax.psum(partial_grad, "node")


def shards(
    features, upstream, weight_one, weight_two, neighbours, edge_weight, fetch_block, fetch_count
):
    peer_count = lax.axis_size("node")
    device = lax.axis_index("node")
    band_matrix, far_matrix, row_total, asked_blocks = edge_tables(
        neighbours, edge_weight, fetch_block, fetch_count, peer_count, device
    )
    grad_scale = 1.0 / math.sqrt(ROWS * peer_count)
    agg_one = aggregate(features, band_matrix, far_matrix, row_total, asked_blocks)
    pre_one = jnp.dot(agg_one, weight_one, preferred_element_type=jnp.float32)
    hidden_f, gelu_back = jax.vjp(gelu_tanh, pre_one)
    hidden = hidden_f.astype(jnp.bfloat16)
    agg_two = aggregate(hidden, band_matrix, far_matrix, row_total, asked_blocks)
    part_two = contract_rows(agg_two, upstream)
    summed_two = sum_weight_grad(part_two)
    q_two = lax.dot_general(
        upstream, weight_two, (((1,), (1,)), ((), ())), preferred_element_type=jnp.float32
    )
    q_two = (q_two / row_total[:, None]).astype(jnp.bfloat16)
    back_hidden = adjoint(q_two, band_matrix, far_matrix, asked_blocks, peer_count)
    d_pre = gelu_back(back_hidden)[0].astype(jnp.bfloat16)
    part_one = contract_rows(agg_one, d_pre)
    summed_one = sum_weight_grad(part_one)
    q_one = lax.dot_general(
        d_pre, weight_one, (((1,), (1,)), ((), ())), preferred_element_type=jnp.float32
    )
    q_one = (q_one / row_total[:, None]).astype(jnp.bfloat16)
    d_features = adjoint(q_one, band_matrix, far_matrix, asked_blocks, peer_count)
    grad_one = (summed_one * grad_scale).astype(jnp.bfloat16)
    grad_two = (summed_two * grad_scale).astype(jnp.bfloat16)
    return (d_features.astype(jnp.bfloat16), grad_one, grad_two)


def solution(mesh):
    placed = (
        P(("rep", "node"), None),
        P(("rep", "node"), None),
        P(),
        P(),
        P(("rep", "node"), None),
        P(("rep", "node"), None),
        P("rep", None),
        P("rep"),
    )
    return jax.shard_map(
        shards,
        mesh=mesh,
        in_specs=placed,
        out_specs=(P(("rep", "node"), None), P("rep", None), P("rep", None)),
        check_vma=False,
    )
```

profile of v0, /device:TPU:0, one launch (start us, length us, event | category | flops | bytes accessed | tf_op | source)
XLA Modules:
  0.0 309.5 jit_solution(4038717599790663979)
XLA Ops:
  8.6 5.4 %collective-permute-start.2 = (bf16[32,512]{1,0:T(8,128)(2,1)}, bf16[32,512]{1,0:T(8,128)(2,1)}, u32[]{:S(2)}, u32[]{:S(2)}) collective-permute-start(bf16[32,512]{1,0:T(8,128)(2,1)} %get-tuple-element.74), channel_id=1, source_target_pairs={{0,2},{2,4},{4,6},{6,8},{8,10},{10,12},{12,14},{14,16},{16,18},{18... | collective-permute-start | bytes 98312 | tf_op jit(solution)/shard_map/ppermute | solution.py:20
  17.1 2.2 gather_fusion.2
  19.3 8.0 %all-to-all-start.1 = ((bf16[16,2,8,512]{3,2,1,0:T(8,128)(2,1)}), bf16[16,2,8,512]{3,2,1,0:T(8,128)(2,1)S(1)}, u32[]{:S(2)}, u32[]{:S(2)}) async-start(bf16[16,2,8,512]{3,2,1,0:T(8,128)(2,1)} %bitcast.29), calls=%async_computation.1 | async-start | bytes 524288 | tf_op jit(solution)/shard_map/all_to_all | solution.py:78
  31.9 10.1 %select_select_fusion = s32[128,32]{0,1:T(8,128)S(1)} fusion(s32[128,32]{0,1:T(8,128)S(1)} %get-tuple-element.65, s32[]{:T(128)} %bitcast.5, s32[]{:T(128)} %bitcast.6, s32[]{:T(128)} %bitcast.7, s32[]{:T(128)} %bitcast.8, s32[]{:T(128)} %bitcast.9, s32[]{:T(128)} %bitcast.10, s32[]{:T(128)} %bitcast.11, s32[]{:T(128)} %bitcast.12, s32[]{:T(128)} %bitcast.13, ...), kind=kLoop, calls=%fused_computation.100 | loop fusion | flops 139264 | bytes 32832 | tf_op jit(solution)/shard_map/jit(_take)/select_n | solution.py:42
  42.1 10.8 %gather_fusion = s32[4096,2]{1,0:T(8,128)S(1)} fusion(s32[16,2]{1,0:T(8,128)S(1)} %constant_dynamic-slice_fusion, s32[4096]{0:T(1024)S(1)} %broadcast_clamp_fusion), kind=kCustom, calls=%fused_computation | custom fusion | bytes 81920 | tf_op jit(solution)/shard_map/jit(_take)/gather | solution.py:40
  52.8 6.2 %fusion.57 = (pred[128,32]{1,0:T(8,128)(4,1)}, pred[128,32,2]{2,1,0:T(8,128)(4,1)S(1)}) fusion(s32[128,32]{1,0:T(8,128)S(1)} %copy.64, s32[128,32]{1,0:T(8,128)S(1)} %copy.63, s32[128,32,2]{2,1,0:T(8,128)S(1)} %bitcast.88, pred[128,32]{1,0:T(8,128)(4,1)} %copy.60), kind=kLoop, calls=%fused_computation.136 | loop fusion | flops 36864 | bytes 81920 | tf_op jit(solution)/shard_map/reduce_or | solution.py:45
  60.9 5.1 %iota_reduce_fusion = (pred[128,32]{1,0:T(8,128)(4,1)}, s32[128,32]{1,0:T(8,128)S(1)}) fusion(pred[128,32,2]{2,1,0:T(8,128)(4,1)S(1)} %get-tuple-element.63), kind=kLoop, calls=%fused_computation.9 | loop fusion | flops 28672 | bytes 28672 | tf_op jit(solution)/shard_map/edge_tables/reduce | solution.py:46
  68.6 21.9 %scatter_custom_fusion.3 = f32[24576]{0:T(1024)S(1)} fusion(s32[4096]{0:T(1024)S(1)} %reshape.324, f32[4096]{0:T(1024)S(1)} %reshape.326, f32[]{:T(128)} %constant.212.clone.1), kind=kCustom, calls=%fused_computation.67 | custom fusion | flops 4096 | bytes 98308
  90.6 7.1 %scatter_fusion = f32[128,192]{0,1:T(8,128)S(1)} fusion(f32[128,192]{0,1:T(8,128)S(1)} %bitcast.89, s32[128]{0:T(128)S(1)} %fusion.52, f32[128]{0:T(128)S(1)} %broadcast.327), kind=kCustom, calls=%fused_computation.4 | custom fusion | flops 128 | bytes 2560 | tf_op jit(solution)/shard_map/scatter-add | solution.py:57
  98.3 3.8 %collective-permute-start = (bf16[32,512]{1,0:T(8,128)(2,1)S(1)}, bf16[32,512]{1,0:T(8,128)(2,1)S(1)}, u32[]{:S(2)}, u32[]{:S(2)}) collective-permute-start(bf16[32,512]{1,0:T(8,128)(2,1)S(1)} %get-tuple-element.70), channel_id=1, source_target_pairs={{0,2},{2,4},{4,6},{6,8},{8,10},{10,12},{12,14},{14,16},{16,18},{18... | collective-permute-start | bytes 98312 | tf_op jit(solution)/shard_map/ppermute | solution.py:20
  103.8 28.8 %scatter_custom_fusion.4 = f32[32768]{0:T(1024)S(1)} fusion(s32[4096]{0:T(1024)S(1)} %reshape.330, f32[4096]{0:T(1024)S(1)} %reshape.332, f32[]{:T(128)} %constant.212.clone.1), kind=kCustom, calls=%fused_computation.65 | custom fusion | flops 4096 | bytes 131076
  133.6 7.7 %all-to-all-start = ((bf16[16,2,8,512]{3,2,1,0:T(8,128)(2,1)}), bf16[16,2,8,512]{3,2,1,0:T(8,128)(2,1)S(1)}, u32[]{:S(2)}, u32[]{:S(2)}) async-start(bf16[16,2,8,512]{3,2,1,0:T(8,128)(2,1)} %bitcast.25), calls=%async_computation | async-start | bytes 524288 | tf_op jit(solution)/shard_map/all_to_all | solution.py:99
  142.8 7.0 %all-to-all-done = bf16[16,2,8,512]{3,2,1,0:T(8,128)(2,1)S(1)} async-done(((bf16[16,2,8,512]{3,2,1,0:T(8,128)(2,1)}), bf16[16,2,8,512]{3,2,1,0:T(8,128)(2,1)S(1)}, u32[]{:S(2)}, u32[]{:S(2)}) %all-to-all-start) | async-done | bytes 262176 | tf_op jit(solution)/shard_map/all_to_all | solution.py:99
  149.9 1.9 scatter_fusion.1
  153.2 3.5 %all-to-all-start.3 = ((bf16[16,2,8,512]{3,2,1,0:T(8,128)(2,1)}), bf16[16,2,8,512]{3,2,1,0:T(8,128)(2,1)S(1)}, u32[]{:S(2)}, u32[]{:S(2)}) async-start(bf16[16,2,8,512]{3,2,1,0:T(8,128)(2,1)} %bitcast.36), calls=%async_computation.3 | async-start | bytes 524288 | tf_op jit(solution)/shard_map/all_to_all | solution.py:78
  156.8 3.8 %collective-permute-start.6 = (bf16[32,512]{1,0:T(8,128)(2,1)S(1)}, bf16[32,512]{1,0:T(8,128)(2,1)S(1)}, u32[]{:S(2)}, u32[]{:S(2)}) collective-permute-start(bf16[32,512]{1,0:T(8,128)(2,1)S(1)} %get-tuple-element.72), channel_id=1, source_target_pairs={{0,2},{2,4},{4,6},{6,8},{8,10},{10,12},{12,14},{14,16},{16,18},{18... | collective-permute-start | bytes 98312 | tf_op jit(solution)/shard_map/ppermute | solution.py:20
  163.3 2.0 all-to-all-done.3
  169.3 7.3 %all-to-all-start.2 = ((bf16[16,2,8,512]{3,2,1,0:T(8,128)(2,1)}), bf16[16,2,8,512]{3,2,1,0:T(8,128)(2,1)S(1)}, u32[]{:S(2)}, u32[]{:S(2)}) async-start(bf16[16,2,8,512]{3,2,1,0:T(8,128)(2,1)} %bitcast.32), calls=%async_computation.2 | async-start | bytes 524288 | tf_op jit(solution)/shard_map/all_to_all | solution.py:99
  176.8 3.8 %collective-permute-start.4 = (bf16[32,512]{1,0:T(8,128)(2,1)S(1)}, bf16[32,512]{1,0:T(8,128)(2,1)S(1)}, u32[]{:S(2)}, u32[]{:S(2)}) collective-permute-start(bf16[32,512]{1,0:T(8,128)(2,1)S(1)} %get-tuple-element.68), channel_id=1, source_target_pairs={{0,2},{2,4},{4,6},{6,8},{8,10},{10,12},{12,14},{14,16},{16,18},{18... | collective-permute-start | bytes 98312 | tf_op jit(solution)/shard_map/ppermute | solution.py:20
  182.7 3.9 %collective-permute-done.5 = bf16[32,512]{1,0:T(8,128)(2,1)S(1)} collective-permute-done((bf16[32,512]{1,0:T(8,128)(2,1)S(1)}, bf16[32,512]{1,0:T(8,128)(2,1)S(1)}, u32[]{:S(2)}, u32[]{:S(2)}) %collective-permute-start.5) | collective-permute-done | bytes 32800 | tf_op jit(solution)/shard_map/ppermute | solution.py:23
  186.7 2.6 all-to-all-done.2
  189.4 1.9 scatter_fusion.2
  191.9 107.6 %all-reduce.3.cloned.1.call-done = (f32[512,512]{1,0:T(8,128)}, f32[512,512]{1,0:T(8,128)}) async-done(((f32[512,512]{1,0:T(8,128)}, f32[512,512]{1,0:T(8,128)}), (f32[512,512]{1,0:T(8,128)}, f32[512,512]{1,0:T(8,128)})) %all-reduce.3.cloned.1.call-update) | async-done | bytes 2097168 | tf_op jit(solution)/shard_map/psum | solution.py:113
  299.5 2.2 multiply_convert_fusion.1
  (99 shorter events, 30.2 us)
Async XLA Ops:
  7.2 135.4 %copy-start = (bf16[512,512]{1,0:T(8,128)(2,1)S(1)}, bf16[512,512]{1,0:T(8,128)(2,1)}, u32[]{:S(2)}) copy-start(bf16[512,512]{1,0:T(8,128)(2,1)} %param.18) | copy-start | bytes 1572868
  8.6 132.9 %collective-permute-start.2 = (bf16[32,512]{1,0:T(8,128)(2,1)}, bf16[32,512]{1,0:T(8,128)(2,1)}, u32[]{:S(2)}, u32[]{:S(2)}) collective-permute-start(bf16[32,512]{1,0:T(8,128)(2,1)} %get-tuple-element.74), channel_id=1, source_target_pairs={{0,2},{2,4},{4,6},{6,8},{8,10},{10,12},{12,14},{14,16},{16,18},{18... | collective-permute-start | bytes 98312 | tf_op jit(solution)/shard_map/ppermute | solution.py:20
  14.1 127.5 %collective-permute-start.3 = (bf16[32,512]{1,0:T(8,128)(2,1)}, bf16[32,512]{1,0:T(8,128)(2,1)}, u32[]{:S(2)}, u32[]{:S(2)}) collective-permute-start(bf16[32,512]{1,0:T(8,128)(2,1)} %get-tuple-element.75), channel_id=1, source_target_pairs={{2,0},{4,2},{6,4},{8,6},{10,8},{12,10},{14,12},{16,14},{18,16},{20... | collective-permute-start | bytes 98312 | tf_op jit(solution)/shard_map/ppermute | solution.py:23
  17.1 10.2 %copy-start.4 = (s32[1024]{0:T(1024)}, s32[1024]{0:T(1024)S(1)}, u32[]{:S(2)}) copy-start(s32[1024]{0:T(1024)S(1)} %pad_clamp_fusion) | copy-start | bytes 12292
  19.3 114.4 %all-to-all-start.1 = ((bf16[16,2,8,512]{3,2,1,0:T(8,128)(2,1)}), bf16[16,2,8,512]{3,2,1,0:T(8,128)(2,1)S(1)}, u32[]{:S(2)}, u32[]{:S(2)}) async-start(bf16[16,2,8,512]{3,2,1,0:T(8,128)(2,1)} %bitcast.29), calls=%async_computation.1 | async-start | bytes 524288 | tf_op jit(solution)/shard_map/all_to_all | solution.py:78
  59.0 38.7 %copy-start.3 = (bf16[128,512]{1,0:T(8,128)(2,1)S(1)}, bf16[128,512]{1,0:T(8,128)(2,1)}, u32[]{:S(2)}) copy-start(bf16[128,512]{1,0:T(8,128)(2,1)} %param.17) | copy-start | bytes 393220
  59.0 38.7 %copy-start.6 = (bf16[512,512]{1,0:T(8,128)(2,1)S(1)}, bf16[512,512]{1,0:T(8,128)(2,1)}, u32[]{:S(2)}) copy-start(bf16[512,512]{1,0:T(8,128)(2,1)} %param.19) | copy-start | bytes 1572868
  98.1 43.5 %copy-start.2 = (bf16[128,512]{1,0:T(8,128)(2,1)S(1)}, bf16[128,512]{1,0:T(8,128)(2,1)}, u32[]{:S(2)}) copy-start(bf16[128,512]{1,0:T(8,128)(2,1)} %param.16) | copy-start | bytes 393220
  98.3 35.3 %collective-permute-start = (bf16[32,512]{1,0:T(8,128)(2,1)S(1)}, bf16[32,512]{1,0:T(8,128)(2,1)S(1)}, u32[]{:S(2)}, u32[]{:S(2)}) collective-permute-start(bf16[32,512]{1,0:T(8,128)(2,1)S(1)} %get-tuple-element.70), channel_id=1, source_target_pairs={{0,2},{2,4},{4,6},{6,8},{8,10},{10,12},{12,14},{14,16},{16,18},{18... | collective-permute-start | bytes 98312 | tf_op jit(solution)/shard_map/ppermute | solution.py:20
  102.1 31.5 %collective-permute-start.1 = (bf16[32,512]{1,0:T(8,128)(2,1)S(1)}, bf16[32,512]{1,0:T(8,128)(2,1)S(1)}, u32[]{:S(2)}, u32[]{:S(2)}) collective-permute-start(bf16[32,512]{1,0:T(8,128)(2,1)S(1)} %get-tuple-element.71), channel_id=1, source_target_pairs={{2,0},{4,2},{6,4},{8,6},{10,8},{12,10},{14,12},{16,14},{18,16},{20... | collective-permute-start | bytes 98312 | tf_op jit(solution)/shard_map/ppermute | solution.py:23
  133.6 16.2 %all-to-all-start = ((bf16[16,2,8,512]{3,2,1,0:T(8,128)(2,1)}), bf16[16,2,8,512]{3,2,1,0:T(8,128)(2,1)S(1)}, u32[]{:S(2)}, u32[]{:S(2)}) async-start(bf16[16,2,8,512]{3,2,1,0:T(8,128)(2,1)} %bitcast.25), calls=%async_computation | async-start | bytes 524288 | tf_op jit(solution)/shard_map/all_to_all | solution.py:99
  142.5 9.4 %copy-start.5 = (s32[1024]{0:T(1024)S(1)}, s32[1024]{0:T(1024)}, u32[]{:S(2)}) copy-start(s32[1024]{0:T(1024)} %copy-done.4) | copy-start | bytes 12292
  153.2 12.0 %all-to-all-start.3 = ((bf16[16,2,8,512]{3,2,1,0:T(8,128)(2,1)}), bf16[16,2,8,512]{3,2,1,0:T(8,128)(2,1)S(1)}, u32[]{:S(2)}, u32[]{:S(2)}) async-start(bf16[16,2,8,512]{3,2,1,0:T(8,128)(2,1)} %bitcast.36), calls=%async_computation.3 | async-start | bytes 524288 | tf_op jit(solution)/shard_map/all_to_all | solution.py:78
  156.8 142.7 %all-reduce.3.cloned.1.call-start = ((), (), s32[]{:S(2)}) async-start(), calls=%async_computation.4 | async-start | bytes 4194304 | tf_op jit(solution)/shard_map/psum | solution.py:113
  156.8 8.6 %collective-permute-start.6 = (bf16[32,512]{1,0:T(8,128)(2,1)S(1)}, bf16[32,512]{1,0:T(8,128)(2,1)S(1)}, u32[]{:S(2)}, u32[]{:S(2)}) collective-permute-start(bf16[32,512]{1,0:T(8,128)(2,1)S(1)} %get-tuple-element.72), channel_id=1, source_target_pairs={{0,2},{2,4},{4,6},{6,8},{8,10},{10,12},{12,14},{14,16},{16,18},{18... | collective-permute-start | bytes 98312 | tf_op jit(solution)/shard_map/ppermute | solution.py:20
  160.7 5.8 %collective-permute-start.7 = (bf16[32,512]{1,0:T(8,128)(2,1)S(1)}, bf16[32,512]{1,0:T(8,128)(2,1)S(1)}, u32[]{:S(2)}, u32[]{:S(2)}) collective-permute-start(bf16[32,512]{1,0:T(8,128)(2,1)S(1)} %get-tuple-element.73), channel_id=1, source_target_pairs={{2,0},{4,2},{6,4},{8,6},{10,8},{12,10},{14,12},{16,14},{18,16},{20... | collective-permute-start | bytes 98312 | tf_op jit(solution)/shard_map/ppermute | solution.py:23
  169.3 20.0 %all-to-all-start.2 = ((bf16[16,2,8,512]{3,2,1,0:T(8,128)(2,1)}), bf16[16,2,8,512]{3,2,1,0:T(8,128)(2,1)S(1)}, u32[]{:S(2)}, u32[]{:S(2)}) async-start(bf16[16,2,8,512]{3,2,1,0:T(8,128)(2,1)} %bitcast.32), calls=%async_computation.2 | async-start | bytes 524288 | tf_op jit(solution)/shard_map/all_to_all | solution.py:99
  176.8 5.9 %collective-permute-start.4 = (bf16[32,512]{1,0:T(8,128)(2,1)S(1)}, bf16[32,512]{1,0:T(8,128)(2,1)S(1)}, u32[]{:S(2)}, u32[]{:S(2)}) collective-permute-start(bf16[32,512]{1,0:T(8,128)(2,1)S(1)} %get-tuple-element.68), channel_id=1, source_target_pairs={{0,2},{2,4},{4,6},{6,8},{8,10},{10,12},{12,14},{14,16},{16,18},{18... | collective-permute-start | bytes 98312 | tf_op jit(solution)/shard_map/ppermute | solution.py:20
  180.7 6.0 %collective-permute-start.5 = (bf16[32,512]{1,0:T(8,128)(2,1)S(1)}, bf16[32,512]{1,0:T(8,128)(2,1)S(1)}, u32[]{:S(2)}, u32[]{:S(2)}) collective-permute-start(bf16[32,512]{1,0:T(8,128)(2,1)S(1)} %get-tuple-element.69), channel_id=1, source_target_pairs={{2,0},{4,2},{6,4},{8,6},{10,8},{12,10},{14,12},{16,14},{18,16},{20... | collective-permute-start | bytes 98312 | tf_op jit(solution)/shard_map/ppermute | solution.py:23
  299.5 2.2 copy-start.1
Sparse Core Ops, SparseCore 0:
  168.1 131.2 all-reduce.2
where the time goes:
time: 311 us; the launch traced here: 309 us
  waiting for transfers between devices  125 us (40%)
  other arithmetic  92.5 us (30%)
  starting transfers between devices  48.7 us (16%)
  local copies, waits for them, and re-layouts  21.6 us (7%)
  between operations  14.6 us (5%)
  matrix products  7.27 us (2%)
    psum x1, waiting for transfers between devices, sum_weight_grad(): return lax.psum(partial_grad, 'node')  108 us
    unnamed x5, other arithmetic  52.4 us
    ppermute x4, starting transfers between devices, with_halo(): lax.ppermute(lax.slice_in_dim(block, block.shape[dim] - width, None, axis...  16.9 us
    all_to_all x2, starting transfers between devices, adjoint(): lax.all_to_all(back_far.astype(jnp.bfloat16), 'node', split_axis=0, conca...  15 us
    all_to_all x2, starting transfers between devices, aggregate(): lax.all_to_all(outgoing, 'node', split_axis=0, concat_axis=0, tiled=True)  11.6 us
    gather x1, local copies, waits for them, and re-layouts, edge_tables(): listed = jnp.take(my_table, owner_dev, axis=0)  10.8 us
    select_n x1, other arithmetic, edge_tables(): jnp.take(my_counts, owner_dev)[..., None]  10.1 us
    all_to_all x2, waiting for transfers between devices, adjoint(): lax.all_to_all(back_far.astype(jnp.bfloat16), 'node', split_axis=0, conca...  9.64 us
  transfers between devices with their start and end apart: 13, of which 7 were waited for; matrix products, arithmetic and copies ran while one was open for 36% of the time, Pallas kernels for 0%

commit v1 on v0

--- a/solution.py
+++ b/solution.py
@@ -110,7 +110,7 @@
 
 
 def sum_weight_grad(partial_grad):
-    return lax.psum(partial_grad, "node")
+    return jnp.sum(lax.all_gather(partial_grad, axis_name="node"), axis=0)
 
 
 def shards(

time: 311 us -> 560 us (1.80)
  waiting for transfers between devices: 125 us -> 359 us
  other arithmetic: 92.5 us -> 107 us
    all_gather x0 -> x2, waiting for transfers between devices: none -> 340 us  [sum_weight_grad(): return jnp.sum(lax.all_gather(partial_grad, axis_name='node'), axis=0)]
    psum x1 -> x0, waiting for transfers between devices: 108 us -> none  [sum_weight_grad(): return lax.psum(partial_grad, 'node')]
    reduce_sum x0 -> x2, other arithmetic: none -> 15.8 us  [sum_weight_grad(): return jnp.sum(lax.all_gather(partial_grad, axis_name='node'), axis=0)]
  transfers between devices with their start and end apart: 13 -> 14, of which waited for: 7 -> 8; matrix products, arithmetic and copies ran while one was open for 36% -> 22% of each run, Pallas kernels for 0% -> 0%
where the time goes in v1:
time: 560 us; the launch traced here: 559 us
  waiting for transfers between devices  359 us (64%)
  other arithmetic  107 us (19%)
  starting transfers between devices  49 us (9%)
  local copies, waits for them, and re-layouts  21.6 us (4%)
  between operations  14.6 us (3%)
  matrix products  7.3 us (1%)
    all_gather x2, waiting for transfers between devices, sum_weight_grad(): return jnp.sum(lax.all_gather(partial_grad, axis_name='node'), axis=0)  340 us
    unnamed x5, other arithmetic  52.4 us
    ppermute x4, starting transfers between devices, with_halo(): lax.ppermute(lax.slice_in_dim(block, block.shape[dim] - width, None, axis...  16.9 us
    reduce_sum x2, other arithmetic, sum_weight_grad(): return jnp.sum(lax.all_gather(partial_grad, axis_name='node'), axis=0)  15.8 us
    all_to_all x2, starting transfers between devices, adjoint(): lax.all_to_all(back_far.astype(jnp.bfloat16), 'node', split_axis=0, conca...  15.1 us
    all_to_all x2, starting transfers between devices, aggregate(): lax.all_to_all(outgoing, 'node', split_axis=0, concat_axis=0, tiled=True)  11.6 us
  transfers between devices with their start and end apart: 14, of which 8 were waited for; matrix products, arithmetic and copies ran while one was open for 22% of the time, Pallas kernels for 0%

profile of v1, /device:TPU:0, one launch (start us, length us, event | category | flops | bytes accessed | tf_op | source)
XLA Modules:
  0.0 558.8 jit_solution(2945809125494404508)
XLA Ops:
  8.6 5.4 collective-permute-start.2
  17.1 2.2 gather_fusion.2
  19.3 8.0 %all-to-all-start.1 = ((bf16[16,2,8,512]{3,2,1,0:T(8,128)(2,1)}), bf16[16,2,8,512]{3,2,1,0:T(8,128)(2,1)S(1)}, u32[]{:S(2)}, u32[]{:S(2)}) async-start(bf16[16,2,8,512]{3,2,1,0:T(8,128)(2,1)} %bitcast.29), calls=%async_computation.1 | async-start | bytes 524288 | tf_op jit(solution)/shard_map/all_to_all | solution.py:78
  31.9 10.0 %select_select_fusion = s32[128,32]{0,1:T(8,128)S(1)} fusion(s32[128,32]{0,1:T(8,128)S(1)} %get-tuple-element.63, s32[]{:T(128)} %bitcast.5, s32[]{:T(128)} %bitcast.6, s32[]{:T(128)} %bitcast.7, s32[]{:T(128)} %bitcast.8, s32[]{:T(128)} %bitcast.9, s32[]{:T(128)} %bitcast.10, s32[]{:T(128)} %bitcast.11, s32[]{:T(128)} %bitcast.12, s32[]{:T(128)} %bitcast.13, ...), kind=kLoop, calls=%fused_computation.100 | loop fusion | flops 139264 | bytes 32832 | tf_op jit(solution)/shard_map/jit(_take)/select_n | solution.py:42
  42.0 10.8 %gather_fusion = s32[4096,2]{1,0:T(8,128)S(1)} fusion(s32[16,2]{1,0:T(8,128)S(1)} %constant_dynamic-slice_fusion, s32[4096]{0:T(1024)S(1)} %broadcast_clamp_fusion), kind=kCustom, calls=%fused_computation | custom fusion | bytes 81920 | tf_op jit(solution)/shard_map/jit(_take)/gather | solution.py:40
  52.8 6.2 %fusion.57 = (pred[128,32]{1,0:T(8,128)(4,1)}, pred[128,32,2]{2,1,0:T(8,128)(4,1)S(1)}) fusion(s32[128,32]{1,0:T(8,128)S(1)} %copy.64, s32[128,32]{1,0:T(8,128)S(1)} %copy.63, s32[128,32,2]{2,1,0:T(8,128)S(1)} %bitcast.92, pred[128,32]{1,0:T(8,128)(4,1)} %copy.60), kind=kLoop, calls=%fused_computation.136 | loop fusion | flops 36864 | bytes 81920 | tf_op jit(solution)/shard_map/reduce_or | solution.py:45
  60.8 5.1 iota_reduce_fusion
  68.6 21.9 %scatter_custom_fusion.3 = f32[24576]{0:T(1024)S(1)} fusion(s32[4096]{0:T(1024)S(1)} %reshape.324, f32[4096]{0:T(1024)S(1)} %reshape.326, f32[]{:T(128)} %constant.212.clone.1), kind=kCustom, calls=%fused_computation.67 | custom fusion | flops 4096 | bytes 98308
  90.5 7.1 %scatter_fusion = f32[128,192]{0,1:T(8,128)S(1)} fusion(f32[128,192]{0,1:T(8,128)S(1)} %bitcast.93, s32[128]{0:T(128)S(1)} %fusion.52, f32[128]{0:T(128)S(1)} %broadcast.327), kind=kCustom, calls=%fused_computation.4 | custom fusion | flops 128 | bytes 2560 | tf_op jit(solution)/shard_map/scatter-add | solution.py:57
  98.2 3.8 collective-permute-start
  103.7 28.8 %scatter_custom_fusion.4 = f32[32768]{0:T(1024)S(1)} fusion(s32[4096]{0:T(1024)S(1)} %reshape.330, f32[4096]{0:T(1024)S(1)} %reshape.332, f32[]{:T(128)} %constant.212.clone.1), kind=kCustom, calls=%fused_computation.65 | custom fusion | flops 4096 | bytes 131076
  133.6 7.7 %all-to-all-start = ((bf16[16,2,8,512]{3,2,1,0:T(8,128)(2,1)}), bf16[16,2,8,512]{3,2,1,0:T(8,128)(2,1)S(1)}, u32[]{:S(2)}, u32[]{:S(2)}) async-start(bf16[16,2,8,512]{3,2,1,0:T(8,128)(2,1)} %bitcast.25), calls=%async_computation | async-start | bytes 524288 | tf_op jit(solution)/shard_map/all_to_all | solution.py:99
  142.9 6.8 %all-to-all-done = bf16[16,2,8,512]{3,2,1,0:T(8,128)(2,1)S(1)} async-done(((bf16[16,2,8,512]{3,2,1,0:T(8,128)(2,1)}), bf16[16,2,8,512]{3,2,1,0:T(8,128)(2,1)S(1)}, u32[]{:S(2)}, u32[]{:S(2)}) %all-to-all-start) | async-done | bytes 262176 | tf_op jit(solution)/shard_map/all_to_all | solution.py:99
  154.5 3.5 all-to-all-start.3
  158.1 3.8 collective-permute-start.6
  163.2 3.6 all-to-all-done.3
  171.2 7.5 %all-to-all-start.2 = ((bf16[16,2,8,512]{3,2,1,0:T(8,128)(2,1)}), bf16[16,2,8,512]{3,2,1,0:T(8,128)(2,1)S(1)}, u32[]{:S(2)}, u32[]{:S(2)}) async-start(bf16[16,2,8,512]{3,2,1,0:T(8,128)(2,1)} %bitcast.32), calls=%async_computation.2 | async-start | bytes 524288 | tf_op jit(solution)/shard_map/all_to_all | solution.py:99
  178.9 3.8 collective-permute-start.4
  184.3 4.3 collective-permute-done.5
  188.7 3.0 all-to-all-done.2
  194.2 156.3 %all-gather.5.cloned.1.call-done = f32[8192,512]{1,0:T(8,128)} async-done(((f32[512,512]{1,0:T(8,128)}), f32[8192,512]{1,0:T(8,128)}) %all-gather.5.cloned.1.call-update) | async-done | bytes 16777232 | tf_op jit(solution)/shard_map/all_gather | solution.py:113
  350.5 7.9 %reduce_sum.28 = f32[512,512]{1,0:T(8,128)S(1)} reduce(f32[16,512,512]{2,1,0:T(8,128)} %bitcast.90, f32[]{:T(128)} %constant.212.clone.1), dimensions={0}, to_apply=%region_8.9 | reduce | flops 3932160 | bytes 17825796 | tf_op jit(solution)/shard_map/reduce_sum | solution.py:113
  359.4 183.8 %all-gather.7.cloned.1.call-done = f32[8192,512]{1,0:T(8,128)} async-done(((f32[512,512]{1,0:T(8,128)}), f32[8192,512]{1,0:T(8,128)}) %all-gather.7.cloned.1.call-update) | async-done | bytes 16777232 | tf_op jit(solution)/shard_map/all_gather | solution.py:113
  543.1 7.9 %reduce_sum.29 = f32[512,512]{1,0:T(8,128)S(1)} reduce(f32[16,512,512]{2,1,0:T(8,128)} %bitcast.91, f32[]{:T(128)} %constant.212.clone.1), dimensions={0}, to_apply=%region_9.10 | reduce | flops 3932160 | bytes 17825796 | tf_op jit(solution)/shard_map/reduce_sum | solution.py:113
  (104 shorter events, 35.0 us)
Async XLA Ops:
  7.2 135.5 %copy-start = (bf16[512,512]{1,0:T(8,128)(2,1)S(1)}, bf16[512,512]{1,0:T(8,128)(2,1)}, u32[]{:S(2)}) copy-start(bf16[512,512]{1,0:T(8,128)(2,1)} %param.18) | copy-start | bytes 1572868
  8.6 133.0 %collective-permute-start.2 = (bf16[32,512]{1,0:T(8,128)(2,1)}, bf16[32,512]{1,0:T(8,128)(2,1)}, u32[]{:S(2)}, u32[]{:S(2)}) collective-permute-start(bf16[32,512]{1,0:T(8,128)(2,1)} %get-tuple-element.72), channel_id=1, source_target_pairs={{0,2},{2,4},{4,6},{6,8},{8,10},{10,12},{12,14},{14,16},{16,18},{18... | collective-permute-start | bytes 98312 | tf_op jit(solution)/shard_map/ppermute | solution.py:20
  14.1 127.6 %collective-permute-start.3 = (bf16[32,512]{1,0:T(8,128)(2,1)}, bf16[32,512]{1,0:T(8,128)(2,1)}, u32[]{:S(2)}, u32[]{:S(2)}) collective-permute-start(bf16[32,512]{1,0:T(8,128)(2,1)} %get-tuple-element.73), channel_id=1, source_target_pairs={{2,0},{4,2},{6,4},{8,6},{10,8},{12,10},{14,12},{16,14},{18,16},{20... | collective-permute-start | bytes 98312 | tf_op jit(solution)/shard_map/ppermute | solution.py:23
  17.1 10.2 %copy-start.3 = (s32[1024]{0:T(1024)}, s32[1024]{0:T(1024)S(1)}, u32[]{:S(2)}) copy-start(s32[1024]{0:T(1024)S(1)} %pad_clamp_fusion) | copy-start | bytes 12292
  19.3 114.3 %all-to-all-start.1 = ((bf16[16,2,8,512]{3,2,1,0:T(8,128)(2,1)}), bf16[16,2,8,512]{3,2,1,0:T(8,128)(2,1)S(1)}, u32[]{:S(2)}, u32[]{:S(2)}) async-start(bf16[16,2,8,512]{3,2,1,0:T(8,128)(2,1)} %bitcast.29), calls=%async_computation.1 | async-start | bytes 524288 | tf_op jit(solution)/shard_map/all_to_all | solution.py:78
  52.8 14.0 %copy-start.5 = (s32[2]{0:T(128)S(1)}, s32[2]{0:T(128)}, u32[]{:S(2)}) copy-start(s32[2]{0:T(128)} %constant.253) | copy-start | bytes 28
  59.0 38.7 %copy-start.2 = (bf16[128,512]{1,0:T(8,128)(2,1)S(1)}, bf16[128,512]{1,0:T(8,128)(2,1)}, u32[]{:S(2)}) copy-start(bf16[128,512]{1,0:T(8,128)(2,1)} %param.17) | copy-start | bytes 393220
  59.0 38.7 %copy-start.6 = (bf16[512,512]{1,0:T(8,128)(2,1)S(1)}, bf16[512,512]{1,0:T(8,128)(2,1)}, u32[]{:S(2)}) copy-start(bf16[512,512]{1,0:T(8,128)(2,1)} %param.19) | copy-start | bytes 1572868
  98.0 43.7 %copy-start.1 = (bf16[128,512]{1,0:T(8,128)(2,1)S(1)}, bf16[128,512]{1,0:T(8,128)(2,1)}, u32[]{:S(2)}) copy-start(bf16[128,512]{1,0:T(8,128)(2,1)} %param.16) | copy-start | bytes 393220
  98.2 35.3 %collective-permute-start = (bf16[32,512]{1,0:T(8,128)(2,1)S(1)}, bf16[32,512]{1,0:T(8,128)(2,1)S(1)}, u32[]{:S(2)}, u32[]{:S(2)}) collective-permute-start(bf16[32,512]{1,0:T(8,128)(2,1)S(1)} %get-tuple-element.68), channel_id=1, source_target_pairs={{0,2},{2,4},{4,6},{6,8},{8,10},{10,12},{12,14},{14,16},{16,18},{18... | collective-permute-start | bytes 98312 | tf_op jit(solution)/shard_map/ppermute | solution.py:20
  102.0 31.5 %collective-permute-start.1 = (bf16[32,512]{1,0:T(8,128)(2,1)S(1)}, bf16[32,512]{1,0:T(8,128)(2,1)S(1)}, u32[]{:S(2)}, u32[]{:S(2)}) collective-permute-start(bf16[32,512]{1,0:T(8,128)(2,1)S(1)} %get-tuple-element.69), channel_id=1, source_target_pairs={{2,0},{4,2},{6,4},{8,6},{10,8},{12,10},{14,12},{16,14},{18,16},{20... | collective-permute-start | bytes 98312 | tf_op jit(solution)/shard_map/ppermute | solution.py:23
  133.6 16.2 %all-to-all-start = ((bf16[16,2,8,512]{3,2,1,0:T(8,128)(2,1)}), bf16[16,2,8,512]{3,2,1,0:T(8,128)(2,1)S(1)}, u32[]{:S(2)}, u32[]{:S(2)}) async-start(bf16[16,2,8,512]{3,2,1,0:T(8,128)(2,1)} %bitcast.25), calls=%async_computation | async-start | bytes 524288 | tf_op jit(solution)/shard_map/all_to_all | solution.py:99
  141.2 209.3 %all-gather.5.cloned.1.call-start = ((), (), s32[]{:S(2)}) async-start(), calls=%async_computation.4 | async-start | bytes 17825792 | tf_op jit(solution)/shard_map/all_gather | solution.py:113
  149.8 3.4 copy-start.4
  154.5 12.4 %all-to-all-start.3 = ((bf16[16,2,8,512]{3,2,1,0:T(8,128)(2,1)}), bf16[16,2,8,512]{3,2,1,0:T(8,128)(2,1)S(1)}, u32[]{:S(2)}, u32[]{:S(2)}) async-start(bf16[16,2,8,512]{3,2,1,0:T(8,128)(2,1)} %bitcast.37), calls=%async_computation.3 | async-start | bytes 524288 | tf_op jit(solution)/shard_map/all_to_all | solution.py:78
  158.1 385.1 %all-gather.7.cloned.1.call-start = ((), (), s32[]{:S(2)}) async-start(), calls=%async_computation.5 | async-start | bytes 17825792 | tf_op jit(solution)/shard_map/all_gather | solution.py:113
  158.1 9.0 %collective-permute-start.6 = (bf16[32,512]{1,0:T(8,128)(2,1)S(1)}, bf16[32,512]{1,0:T(8,128)(2,1)S(1)}, u32[]{:S(2)}, u32[]{:S(2)}) collective-permute-start(bf16[32,512]{1,0:T(8,128)(2,1)S(1)} %get-tuple-element.70), channel_id=1, source_target_pairs={{0,2},{2,4},{4,6},{6,8},{8,10},{10,12},{12,14},{14,16},{16,18},{18... | collective-permute-start | bytes 98312 | tf_op jit(solution)/shard_map/ppermute | solution.py:20
  161.9 6.5 %collective-permute-start.7 = (bf16[32,512]{1,0:T(8,128)(2,1)S(1)}, bf16[32,512]{1,0:T(8,128)(2,1)S(1)}, u32[]{:S(2)}, u32[]{:S(2)}) collective-permute-start(bf16[32,512]{1,0:T(8,128)(2,1)S(1)} %get-tuple-element.71), channel_id=1, source_target_pairs={{2,0},{4,2},{6,4},{8,6},{10,8},{12,10},{14,12},{16,14},{18,16},{20... | collective-permute-start | bytes 98312 | tf_op jit(solution)/shard_map/ppermute | solution.py:23
  171.2 20.4 %all-to-all-start.2 = ((bf16[16,2,8,512]{3,2,1,0:T(8,128)(2,1)}), bf16[16,2,8,512]{3,2,1,0:T(8,128)(2,1)S(1)}, u32[]{:S(2)}, u32[]{:S(2)}) async-start(bf16[16,2,8,512]{3,2,1,0:T(8,128)(2,1)} %bitcast.32), calls=%async_computation.2 | async-start | bytes 524288 | tf_op jit(solution)/shard_map/all_to_all | solution.py:99
  178.9 5.4 collective-permute-start.4
  182.7 5.9 %collective-permute-start.5 = (bf16[32,512]{1,0:T(8,128)(2,1)S(1)}, bf16[32,512]{1,0:T(8,128)(2,1)S(1)}, u32[]{:S(2)}, u32[]{:S(2)}) collective-permute-start(bf16[32,512]{1,0:T(8,128)(2,1)S(1)} %get-tuple-element.67), channel_id=1, source_target_pairs={{2,0},{4,2},{6,4},{8,6},{10,8},{12,10},{14,12},{16,14},{18,16},{20... | collective-permute-start | bytes 98312 | tf_op jit(solution)/shard_map/ppermute | solution.py:23
Sparse Core Ops, SparseCore 0:
  153.3 197.1 all-gather.4
  353.3 189.7 all-gather.6
